TPU v7x, 1024 devices: a whole 4x4x32 slice. The times are simulated.
1024 devices in a mesh: wall: 64 (over x, z_lo), span: 16 (over y, z_hi, core).
Axes of the slice: x: 4, y: 4, z: 32 (z_hi: 2, z_lo: 16; z = z_hi * 16 + z_lo), core: 2. Of those that a mesh axis runs over, the one named last changes fastest.
Arguments:
- velocity: bfloat16 [2, 8, 1536, 4096], P(None, None, 'wall', 'span')
- kx_index: int32 [8], replicated, may hold values from 0 to 5119
- kz_index: int32 [4096], P('span'), may hold values from 0 to 4095
- helm_even: bfloat16 [768, 768], replicated, may hold values from -0.21875 to 0.21875
- helm_odd: bfloat16 [768, 768], replicated, may hold values from -0.21875 to 0.21875
- deriv_even: bfloat16 [768, 768], replicated, may hold values from -0.21875 to 0.21875
- deriv_odd: bfloat16 [768, 768], replicated, may hold values from -0.21875 to 0.21875
Outputs:
- updated: bfloat16 [2, 8, 1536, 4096], P(None, None, 'wall', 'span')
- shear: bfloat16 [2, 8, 1536, 4096], P(None, None, 'wall', 'span')
All inputs are finite; a program needn't handle non-finite values.
Results may differ from a plain program's by a relative error of at most 0.008.
Values may be sent and summed in bfloat16 or wider, within the bound.
A program may use at most 32 MiB of HBM per device.

v0:
```python
import jax
import jax.numpy as jnp
from jax import lax
from jax.sharding import PartitionSpec as P

NY = 1536
KZ = 4096
XMODES = 5120
KX = 8


def line_work(even, odd, helm_even, helm_odd, deriv_even, deriv_odd):
    heven = jnp.einsum("abcj,ij->abci", even, helm_even, preferred_element_type=jnp.float32).astype(
        jnp.bfloat16
    )
    hodd = jnp.einsum("abcj,ij->abci", odd, helm_odd, preferred_element_type=jnp.float32).astype(
        jnp.bfloat16
    )
    dodd = jnp.einsum("abcj,ij->abci", heven, deriv_even, preferred_element_type=jnp.float32)
    deven = jnp.einsum("abcj,ij->abci", hodd, deriv_odd, preferred_element_type=jnp.float32)
    he32 = heven.astype(jnp.float32)
    ho32 = hodd.astype(jnp.float32)
    lines_u = jnp.concatenate([he32 + ho32, (he32 - ho32)[..., ::-1]], axis=-1).astype(jnp.bfloat16)
    lines_d = jnp.concatenate([deven + dodd, (deven - dodd)[..., ::-1]], axis=-1).astype(
        jnp.bfloat16
    )
    return (lines_u, lines_d)


def send_back(lines_u, lines_d):
    planes_u = jnp.swapaxes(lines_u, 2, 3)
    planes_d = jnp.swapaxes(lines_d, 2, 3)
    return (
        lax.all_to_all(planes_u, "wall", split_axis=2, concat_axis=3, tiled=True),
        lax.all_to_all(planes_d, "wall", split_axis=2, concat_axis=3, tiled=True),
    )


def local(velocity, kx_index, kz_index, helm_even, helm_odd, deriv_even, deriv_odd):
    half = NY // 2
    wide = velocity.astype(jnp.float32)
    energy = lax.psum(jnp.sum(wide * wide), ("wall", "span"))
    scale = jnp.float32(2.0 * KX * NY * KZ) / energy
    lines = jnp.swapaxes(
        lax.all_to_all(velocity, "wall", split_axis=3, concat_axis=2, tiled=True), 2, 3
    ).astype(jnp.float32)
    flip = lines[..., ::-1]
    even = ((lines[..., :half] + flip[..., :half]) * 0.5).astype(jnp.bfloat16)
    odd = ((lines[..., :half] - flip[..., :half]) * 0.5).astype(jnp.bfloat16)
    lines_u, lines_d = line_work(even, odd, helm_even, helm_odd, deriv_even, deriv_odd)
    planes_u, planes_d = send_back(lines_u, lines_d)
    kx_sq = (kx_index.astype(jnp.float32) / XMODES) ** 2
    kz_sq = (kz_index.astype(jnp.float32) / KZ) ** 2
    damp = 1.0 / (1.0 + 2.0 * (kx_sq[:, None, None] + kz_sq[None, None, :]))
    factor = scale * damp[None]
    updated = (factor * planes_u.astype(jnp.float32)).astype(jnp.bfloat16)
    shear = (factor * planes_d.astype(jnp.float32)).astype(jnp.bfloat16)
    return (updated, shear)


def solution(mesh):
    in_specs = (P(None, None, "wall", "span"), P(), P("span"), P(), P(), P(), P())
    out_specs = (P(None, None, "wall", "span"), P(None, None, "wall", "span"))
    return jax.shard_map(local, mesh=mesh, in_specs=in_specs, out_specs=out_specs, check_vma=False)
```

profile of v0, /device:TPU:1, one launch (start us, length us, event | category | flops | bytes accessed | tf_op | source)
XLA Modules:
  0.0 340.5 jit_solution(502368173670728059)
XLA Ops:
  0.6 0.0 copy-start
  0.6 2.0 copy.30
  2.6 1.4 reshape.69
  4.0 57.6 %all_to_all.12 = bf16[64,2,768]{2,1,0:T(2,128)(2,1)S(1)} all-to-all(bf16[64,2,768]{2,1,0:T(2,128)(2,1)S(1)} %reshape.69), channel_id=1, replica_groups=mesh['wall'=64,'span'=16] {'wall'}, dimensions={0} | all-to-all | bytes 393216 | tf_op jit(solution)/shard_map/all_to_all | solution.py:45
  61.6 1.5 reshape.70
  63.1 0.8 copy.31
  63.9 0.5 copy.32
  64.5 2.6 copy.33
  67.0 0.0 copy-start.2
  67.0 2.8 reshape.61
  69.9 0.5 slice.13
  70.4 0.0 copy-done.2
  70.4 0.5 fusion.8
  70.9 0.0 copy-done
  70.9 0.0 copy-start.3
  70.9 0.5 convert_subtract_fusion
  71.4 0.8 copy-done.3
  72.2 0.0 copy-start.4
  72.2 0.5 fusion
  72.7 0.8 copy-done.4
  73.4 0.5 fusion.19
  74.0 0.5 rev.8
  74.5 3.6 %copy.37 = bf16[2,8,1536,4]{1,3,0,2:T(4,128)(2,1)} copy(bf16[2,8,1536,4]{2,1,3,0:T(8,128)(2,1)S(1)} %maximum_bitcast_fusion.1) | data formatting | bytes 393216 | tf_op jit(solution)/shard_map/transpose | solution.py:32
  78.2 8.2 %reshape.73 = bf16[64,2,768]{2,1,0:T(2,128)(2,1)} reshape(bf16[1536,2,4,8]{3,2,1,0:T(4,128)(2,1)} %bitcast.60) | data formatting | bytes 393216
  86.4 12.9 %all-to-all-start.2 = ((bf16[64,2,768]{2,1,0:T(2,128)(2,1)}), bf16[64,2,768]{2,1,0:T(2,128)(2,1)S(1)}, u32[]{:S(2)}, u32[]{:S(2)}) async-start(bf16[64,2,768]{2,1,0:T(2,128)(2,1)} %reshape.73), calls=%async_computation.2 | async-start | bytes 393216 | tf_op jit(solution)/shard_map/all_to_all | solution.py:35
  99.3 0.5 rev.7
  99.9 3.6 %copy.34 = bf16[2,8,1536,4]{1,3,0,2:T(4,128)(2,1)} copy(bf16[2,8,1536,4]{2,1,3,0:T(8,128)(2,1)S(1)} %maximum_bitcast_fusion) | data formatting | bytes 393216 | tf_op jit(solution)/shard_map/transpose | solution.py:31
  103.5 0.0 copy-start.5
  103.5 0.0 copy-start.8
  103.5 0.0 copy-start.7
  103.5 8.3 %reshape.71 = bf16[64,2,768]{2,1,0:T(2,128)(2,1)} reshape(bf16[1536,2,4,8]{3,2,1,0:T(4,128)(2,1)} %bitcast.61) | data formatting | bytes 393216
  111.8 15.5 %all-to-all-done.2 = bf16[64,2,768]{2,1,0:T(2,128)(2,1)S(1)} async-done(((bf16[64,2,768]{2,1,0:T(2,128)(2,1)}), bf16[64,2,768]{2,1,0:T(2,128)(2,1)S(1)}, u32[]{:S(2)}, u32[]{:S(2)}) %all-to-all-start.2) | async-done | bytes 196640 | tf_op jit(solution)/shard_map/all_to_all | solution.py:35
  127.3 12.7 %all-to-all-start.1 = ((bf16[64,2,768]{2,1,0:T(2,128)(2,1)}), bf16[64,2,768]{2,1,0:T(2,128)(2,1)S(1)}, u32[]{:S(2)}, u32[]{:S(2)}) async-start(bf16[64,2,768]{2,1,0:T(2,128)(2,1)} %reshape.71), calls=%async_computation.1 | async-start | bytes 393216 | tf_op jit(solution)/shard_map/all_to_all | solution.py:34
  140.0 0.0 copy-done.5
  140.0 0.7 multiply_reduce_fusion
  140.7 163.4 %psum.7 = f32[]{:T(128)} all-reduce(f32[]{:T(128)} %multiply_reduce_fusion), channel_id=1, replica_groups=mesh['wall'=64,'span'=16] {'wall','span'}, use_global_device_ids=true, to_apply=%region_1.0 | all-reduce | flops 1 | bytes 8 | tf_op jit(solution)/shard_map/psum | solution.py:42
  304.8 0.0 copy-done.8
  304.8 0.0 copy-done.7
  304.8 0.1 divide_multiply_fusion
  304.9 0.8 copy.29
  305.7 4.7 %reshape.74 = bf16[1536,2,4,8]{3,2,1,0:T(4,128)(2,1)} reshape(bf16[64,2,768]{2,1,0:T(2,128)(2,1)S(1)} %all-to-all-done.2) | data formatting | bytes 393216
  310.4 4.1 %copy.38 = bf16[2,8,1536,4]{2,1,3,0:T(8,128)(2,1)S(1)} copy(bf16[2,8,1536,4]{1,3,0,2:T(4,128)(2,1)} %bitcast.62) | data formatting | bytes 393216 | tf_op jit(solution)/shard_map/all_to_all | solution.py:35
  314.6 2.9 reshape.63
  317.5 2.8 copy.39
  320.3 0.0 all-to-all-done.1
  320.3 4.8 %reshape.72 = bf16[1536,2,4,8]{3,2,1,0:T(4,128)(2,1)} reshape(bf16[64,2,768]{2,1,0:T(2,128)(2,1)S(1)} %all-to-all-done.1) | data formatting | bytes 393216
  325.1 4.1 %copy.35 = bf16[2,8,1536,4]{2,1,3,0:T(8,128)(2,1)S(1)} copy(bf16[2,8,1536,4]{1,3,0,2:T(4,128)(2,1)} %bitcast.63) | data formatting | bytes 393216 | tf_op jit(solution)/shard_map/all_to_all | solution.py:34
  329.2 2.9 reshape.62
  332.2 0.0 copy-start.6
  332.2 2.8 copy.36
  335.0 0.0 copy-done.6
  335.0 1.7 multiply_convert_fusion
  336.8 0.0 copy-start.1
  336.8 2.5 copy.41
  339.3 0.0 copy-done.1
  339.3 1.3 copy.40
  (7 shorter events, 0.1 us)
Async XLA Ops:
  0.6 70.3 %copy-start = (bf16[768,768]{1,0:T(8,128)(2,1)S(1)}, bf16[768,768]{1,0:T(8,128)(2,1)}, u32[]{:S(2)}) copy-start(bf16[768,768]{1,0:T(8,128)(2,1)} %param.11) | copy-start | bytes 3538948
  67.0 3.3 copy-start.2
  70.9 1.3 copy-start.3
  72.2 1.3 copy-start.4
  86.4 40.9 %all-to-all-start.2 = ((bf16[64,2,768]{2,1,0:T(2,128)(2,1)}), bf16[64,2,768]{2,1,0:T(2,128)(2,1)S(1)}, u32[]{:S(2)}, u32[]{:S(2)}) async-start(bf16[64,2,768]{2,1,0:T(2,128)(2,1)} %reshape.73), calls=%async_computation.2 | async-start | bytes 393216 | tf_op jit(solution)/shard_map/all_to_all | solution.py:35
  103.5 36.5 %copy-start.5 = (bf16[2,8,24,256]{3,2,1,0:T(8,128)(2,1)S(1)}, bf16[2,8,24,256]{3,2,1,0:T(8,128)(2,1)}, u32[]{:S(2)}) copy-start(bf16[2,8,24,256]{3,2,1,0:T(8,128)(2,1)} %param.7) | copy-start | bytes 589828
  103.5 201.3 %copy-start.8 = (s32[8]{0:T(128)S(1)}, s32[8]{0:T(128)}, u32[]{:S(2)}) copy-start(s32[8]{0:T(128)} %param.8) | copy-start | bytes 100
  103.5 201.3 %copy-start.7 = (s32[256]{0:T(256)S(1)}, s32[256]{0:T(256)}, u32[]{:S(2)}) copy-start(s32[256]{0:T(256)} %param.9) | copy-start | bytes 3076
  127.3 193.0 %all-to-all-start.1 = ((bf16[64,2,768]{2,1,0:T(2,128)(2,1)}), bf16[64,2,768]{2,1,0:T(2,128)(2,1)S(1)}, u32[]{:S(2)}, u32[]{:S(2)}) async-start(bf16[64,2,768]{2,1,0:T(2,128)(2,1)} %reshape.71), calls=%async_computation.1 | async-start | bytes 393216 | tf_op jit(solution)/shard_map/all_to_all | solution.py:34
  332.2 2.8 copy-start.6
  336.8 2.5 copy-start.1
where the time goes:
time: 341 us
  blocking collectives  221 us (65%)
  local copies, waits for them, and re-layouts  72.3 us (21%)
  starting transfers between devices  25.5 us (7%)
  waiting for transfers between devices  15.5 us (5%)
    psum x1, blocking collectives, local(): energy = lax.psum(jnp.sum(wide * wide), ('wall', 'span'))  163 us
    all_to_all x1, blocking collectives, local(): lax.all_to_all(velocity, 'wall', split_axis=3, concat_axis=2, tiled=True)  57.6 us
    unnamed x27, local copies, waits for them, and re-layouts  36.2 us
    all_to_all x1, waiting for transfers between devices, send_back(): lax.all_to_all(planes_d, 'wall', split_axis=2, concat_axis=3, tiled=True)  15.5 us
    all_to_all x1, starting transfers between devices, send_back(): lax.all_to_all(planes_d, 'wall', split_axis=2, concat_axis=3, tiled=True)  12.9 us
    all_to_all x1, starting transfers between devices, send_back(): lax.all_to_all(planes_u, 'wall', split_axis=2, concat_axis=3, tiled=True)  12.7 us
  transfers between devices with their start and end apart: 2, of which 1 were waited for; matrix products, arithmetic and copies ran while one was open for 8% of the time, Pallas kernels for 0%

commit v1 on v0

v1 whole, which is shorter than its diff:
```python
import functools

import jax
import jax.numpy as jnp
from jax import lax
from jax.experimental import pallas as pl
from jax.experimental.pallas import tpu as pltpu
from jax.sharding import PartitionSpec as P

NY = 1536
KZ = 4096
XMODES = 5120
KX = 8
HALF = NY // 2
NX = 4
NZ = 16
NB = 24
NL = 128
NC = 2
OWN = NZ * NB
MESH = pl.DeviceIdType.MESH


def kernel(
    v_hbm, kx_ref, kz_ref, he_hbm, ho_hbm, de_hbm, do_hbm,
    outu_ref, outd_ref,
    v_scr, rx, tx, rxo, he, ho, de, do, e1, e2, e3, e4,
    loc_sem, w_sem, zs, zr, xs, xr, bs, br, es1, er1, es2, er2, es3, er3, es4, er4,
):
    f32, bf16 = jnp.float32, jnp.bfloat16
    wall = lax.axis_index("wall")
    span = lax.axis_index("span")
    x, z = wall // NZ, wall % NZ
    yy, zh, core = span // 4, (span // 2) % 2, span % 2
    yc = yy * 2 + core

    def zdev(d):
        return (x * NZ + (z + d) % NZ, span)

    def xdev(d):
        return (((x + d) % NX) * NZ + z, span)

    def ycdev(d):
        t = (yc + d) % 8
        return (wall, ((t // 2) * 2 + zh) * 2 + t % 2)

    hdev = (wall, (yy * 2 + (1 - zh)) * 2 + core)

    vcopies = []
    for h in range(NC):
        c = pltpu.make_async_copy(v_hbm.at[:, :, pl.ds(h * NL, NL)], v_scr.at[h], loc_sem.at[h])
        c.start()
        vcopies.append(c)
    i0 = ((x + 1) // 2 % 2) * OWN
    i0 = pl.multiple_of(i0, OWN)
    wcopies = [
        pltpu.make_async_copy(he_hbm, he, w_sem.at[0]),
        pltpu.make_async_copy(ho_hbm, ho, w_sem.at[1]),
        pltpu.make_async_copy(de_hbm.at[pl.ds(i0, OWN), :], de, w_sem.at[2]),
        pltpu.make_async_copy(do_hbm.at[pl.ds(i0, OWN), :], do, w_sem.at[3]),
    ]
    for c in wcopies:
        c.start()

    barrier = pltpu.get_barrier_semaphore()

    def greet(dev):
        pl.semaphore_signal(barrier, inc=1, device_id=dev, device_id_type=MESH)

    greet(hdev)

    def greet_z(d, carry):
        greet(zdev(d))
        return carry

    lax.fori_loop(1, NZ, greet_z, 0)
    for d in range(1, NX):
        greet(xdev(d))
    for d in range(1, 8):
        greet(ycdev(d))

    for c in vcopies:
        c.wait()
    part = jnp.zeros((8, NL), f32)
    for h in range(NC):
        for c in range(NZ):
            w = v_scr[h, c].astype(f32)
            w = w * w
            part = part + (w[0:8] + w[8:16] + w[16:24])
    e1[yc] = jnp.sum(part, axis=0, keepdims=True)

    pl.semaphore_wait(barrier, 1 + (NZ - 1) + (NX - 1) + 7)

    def zcopy(h, d):
        p = (z + d) % NZ
        return pltpu.make_async_remote_copy(
            src_ref=v_scr.at[h, p], dst_ref=rx.at[h, x * NZ + z],
            send_sem=zs.at[h, d], recv_sem=zr.at[h, z],
            device_id=(x * NZ + p, span), device_id_type=MESH,
        )

    def zwait(h, q):
        pltpu.make_async_remote_copy(
            src_ref=v_scr.at[h, q], dst_ref=rx.at[h, x * NZ + q],
            send_sem=zs.at[h, 0], recv_sem=zr.at[h, q],
            device_id=hdev, device_id_type=MESH,
        ).wait_recv()

    for h in range(NC):
        zcopy(h, 8).start()

        def send_z(m, carry, h=h):
            zcopy(h, 8 - m).start()
            zcopy(h, 8 + m).start()
            return carry

        lax.fori_loop(1, 8, send_z, 0)
        pltpu.make_async_copy(v_scr.at[h, z], rx.at[h, x * NZ + z], zr.at[h, z]).start()

    def ecopy(buf, slot, d, ss, rs, dev):
        return pltpu.make_async_remote_copy(
            src_ref=buf.at[slot], dst_ref=buf.at[slot], send_sem=ss.at[d], recv_sem=rs.at[slot],
            device_id=dev, device_id_type=MESH,
        )

    for d in range(1, 8):
        ecopy(e1, yc, d, es1, er1, ycdev(d)).start()

    rows = lax.broadcasted_iota(jnp.int32, (256, 256), 0)
    cols = lax.broadcasted_iota(jnp.int32, (256, 256), 1)
    flip256 = jnp.where(rows + cols == 255, 1.0, 0.0).astype(bf16)
    flip128 = flip256[0:128, 128:256]
    mirrored = x >= 2
    sign = jnp.where(mirrored, -1.0, 1.0).astype(f32)

    def xcopy(h, d):
        blocks = pl.ds(x * NZ, NZ)
        return pltpu.make_async_remote_copy(
            src_ref=rx.at[h, blocks], dst_ref=rx.at[h, blocks],
            send_sem=xs.at[h, d], recv_sem=xr.at[h, d],
            device_id=xdev(d), device_id_type=MESH,
        )

    def xwait(h, d):
        src = ((x + NX - d) % NX) * NZ
        pltpu.make_async_remote_copy(
            src_ref=rx.at[h, pl.ds(src, NZ)], dst_ref=rx.at[h, pl.ds(src, NZ)],
            send_sem=xs.at[h, d], recv_sem=xr.at[h, d],
            device_id=xdev(d), device_id_type=MESH,
        ).wait_recv()

    def bcopy(h, t, d):
        p = (z + d) % NZ
        return pltpu.make_async_remote_copy(
            src_ref=tx.at[h, t, p], dst_ref=rxo.at[h, t, z],
            send_sem=bs.at[h, t, d], recv_sem=br.at[h, t, z],
            device_id=(x * NZ + p, span), device_id_type=MESH,
        )

    def compute(h):
        lo = rx[h, 0:32].astype(f32).reshape(HALF, NL)
        hi = rx[h, 32:64].astype(f32).reshape(HALF, NL).astype(bf16)
        fl = jnp.concatenate(
            [jnp.dot(flip256, hi[HALF - 256 * (b + 1):HALF - 256 * b], preferred_element_type=f32) for b in range(3)],
            axis=0,
        )
        even = ((lo + fl) * 0.5).astype(bf16)
        odd = ((lo - fl) * 0.5).astype(bf16)
        heven = jnp.dot(he[...], even, preferred_element_type=f32).astype(bf16)
        hodd = jnp.dot(ho[...], odd, preferred_element_type=f32).astype(bf16)
        dodd = jnp.dot(de[...], heven, preferred_element_type=f32)
        deven = jnp.dot(do[...], hodd, preferred_element_type=f32)
        he32, ho32 = heven.astype(f32), hodd.astype(f32)
        upper = i0 > 0
        hes = jnp.where(upper, he32[OWN:], he32[:OWN])
        hos = jnp.where(upper, ho32[OWN:], ho32[:OWN])

        def place(t, lines):
            back = jnp.concatenate(
                [jnp.dot(flip128, lines[OWN - 128 * (b + 1):OWN - 128 * b], preferred_element_type=f32) for b in range(3)],
                axis=0,
            )
            res = jnp.where(mirrored, back, lines.astype(f32))
            tx[h, t] = res.reshape(NZ, NB, NL).astype(bf16)

        place(0, (hes + sign * hos).astype(bf16))
        place(1, (deven + sign * dodd).astype(bf16))

    for h in range(NC):
        lax.fori_loop(0, NZ, lambda q, c, h=h: (zwait(h, q), c)[1], 0)
        for d in range(1, NX):
            xcopy(h, d).start()
        if h == 0:
            for c in wcopies:
                c.wait()
            for d in range(1, 8):
                ecopy(e1, (yc + d) % 8, d, es1, er1, hdev).wait_recv()
            e2[x] = jnp.sum(e1[...], axis=0)
            for d in range(1, NX):
                ecopy(e2, x, d, es2, er2, xdev(d)).start()
        for d in range(1, NX):
            xwait(h, d)
        compute(h)
        for t in range(2):
            bcopy(h, t, 8).start()

            def send_b(m, carry, h=h, t=t):
                bcopy(h, t, 8 - m).start()
                bcopy(h, t, 8 + m).start()
                return carry

            lax.fori_loop(1, 8, send_b, 0)
            pltpu.make_async_copy(tx.at[h, t, z], rxo.at[h, t, z], br.at[h, t, z]).start()
        if h == 0:
            for d in range(1, NX):
                ecopy(e2, (x + d) % NX, d, es2, er2, hdev).wait_recv()
            e3[zh] = jnp.sum(e2[...], axis=0)
            ecopy(e3, zh, 0, es3, er3, hdev).start()
        else:
            ecopy(e3, 1 - zh, 0, es3, er3, hdev).wait_recv()
            e4[z] = jnp.sum(e3[...], axis=0)

            def send_e4(d, carry):
                ecopy(e4, z, d, es4, er4, zdev(d)).start()
                return carry

            lax.fori_loop(1, NZ, send_e4, 0)

    kz = kz_ref[...].astype(f32) / KZ
    kz_sq = kz * kz

    def wait_e4(d, carry):
        ecopy(e4, (z + d) % NZ, d, es4, er4, hdev).wait_recv()
        return carry

    lax.fori_loop(1, NZ, wait_e4, 0)
    energy = jnp.sum(jnp.sum(e4[...], axis=0), axis=1, keepdims=True)
    scale = jnp.float32(2.0 * KX * NY * KZ) / energy
    factors = []
    for k in range(KX):
        kx = kx_ref[k].astype(f32) / XMODES
        factors.append(scale * (1.0 / (1.0 + 2.0 * (kx * kx + kz_sq))))

    def bwait(h, t, c):
        pltpu.make_async_remote_copy(
            src_ref=tx.at[h, t, c], dst_ref=rxo.at[h, t, c],
            send_sem=bs.at[h, t, 0], recv_sem=br.at[h, t, c],
            device_id=hdev, device_id_type=MESH,
        ).wait_recv()

    for h in range(NC):
        for t, out in enumerate((outu_ref, outd_ref)):
            lax.fori_loop(0, NZ, lambda c, carry, h=h, t=t: (bwait(h, t, c), carry)[1], 0)
            for c in range(NZ):
                f = factors[c % KX][:, h * NL:(h + 1) * NL]
                out[c, :, h * NL:(h + 1) * NL] = (f * rxo[h, t, c].astype(f32)).astype(bf16)

    def drain(d, carry):
        for h in range(NC):
            zcopy(h, d).wait_send()
            for t in range(2):
                bcopy(h, t, d).wait_send()
        ecopy(e4, z, d, es4, er4, zdev(d)).wait_send()
        return carry

    lax.fori_loop(1, NZ, drain, 0)
    for d in range(1, NX):
        for h in range(NC):
            xcopy(h, d).wait_send()
        ecopy(e2, x, d, es2, er2, xdev(d)).wait_send()
    for d in range(1, 8):
        ecopy(e1, yc, d, es1, er1, ycdev(d)).wait_send()
    ecopy(e3, zh, 0, es3, er3, hdev).wait_send()


def local(velocity, kx_index, kz_index, helm_even, helm_odd, deriv_even, deriv_odd):
    v = velocity.reshape(NZ, NB, NC * NL)
    vm = pl.BlockSpec(memory_space=pltpu.VMEM)
    hbm = pl.BlockSpec(memory_space=pl.ANY)
    shape = jax.ShapeDtypeStruct((NZ, NB, NC * NL), jnp.bfloat16)
    dma = pltpu.SemaphoreType.DMA
    outu, outd = pl.pallas_call(
        kernel,
        out_shape=(shape, shape),
        in_specs=[hbm, pl.BlockSpec(memory_space=pltpu.SMEM), vm, hbm, hbm, hbm, hbm],
        out_specs=(vm, vm),
        scratch_shapes=[
            pltpu.VMEM((NC, NZ, NB, NL), jnp.bfloat16),
            pltpu.VMEM((NC, NX * NZ, NB, NL), jnp.bfloat16),
            pltpu.VMEM((NC, 2, NZ, NB, NL), jnp.bfloat16),
            pltpu.VMEM((NC, 2, NZ, NB, NL), jnp.bfloat16),
            pltpu.VMEM((HALF, HALF), jnp.bfloat16),
            pltpu.VMEM((HALF, HALF), jnp.bfloat16),
            pltpu.VMEM((OWN, HALF), jnp.bfloat16),
            pltpu.VMEM((OWN, HALF), jnp.bfloat16),
            pltpu.VMEM((8, 1, NL), jnp.float32),
            pltpu.VMEM((NX, 1, NL), jnp.float32),
            pltpu.VMEM((2, 1, NL), jnp.float32),
            pltpu.VMEM((NZ, 1, NL), jnp.float32),
            dma((NC,)), dma((4,)),
            dma((NC, NZ)), dma((NC, NZ)),
            dma((NC, NX)), dma((NC, NX)),
            dma((NC, 2, NZ)), dma((NC, 2, NZ)),
            dma((8,)), dma((8,)), dma((NX,)), dma((NX,)), dma((1,)), dma((2,)), dma((NZ,)), dma((NZ,)),
        ],
        compiler_params=pltpu.CompilerParams(collective_id=0, has_side_effects=True),
    )(v, kx_index, kz_index.reshape(1, NC * NL), helm_even, helm_odd, deriv_even, deriv_odd)
    full = (2, KX, NB, NC * NL)
    return outu.reshape(full), outd.reshape(full)


def solution(mesh):
    in_specs = (P(None, None, "wall", "span"), P(), P("span"), P(), P(), P(), P())
    out_specs = (P(None, None, "wall", "span"), P(None, None, "wall", "span"))
    return jax.shard_map(local, mesh=mesh, in_specs=in_specs, out_specs=out_specs, check_vma=False)
```

time: 341 us -> 99.5 us (0.29)
  the two profiles are of different devices: /device:TPU:1 before, /device:TPU:16 now
where the time goes in v1:
time: 99.5 us; the launch traced here: 99.3 us
  Pallas kernels  95.4 us (96%)
  local copies, waits for them, and re-layouts  3.23 us (3%)
    pallas_call x1, Pallas kernels, local(): pl.pallas_call(kernel, out_shape=(shape, shape), in_specs=[hbm, pl.BlockS...  95.4 us
    unnamed x2, local copies, waits for them, and re-layouts  3.23 us

profile of v1, /device:TPU:16, one launch (start us, length us, event | category | flops | bytes accessed | tf_op | source)
XLA Modules:
  0.0 99.3 jit_solution(6866773251005777888)
XLA Ops:
  0.6 95.4 %shard_map.86 = (bf16[16,24,256]{2,1,0:T(8,128)(2,1)}, bf16[16,24,256]{2,1,0:T(8,128)(2,1)}) custom-call(bf16[16,24,256]{2,1,0:T(8,128)(2,1)} %bitcast.4, s32[8]{0:T(128)} %kx_ref.1, s32[1,256]{1,0:T(1,128)} %bitcast.7, bf16[768,768]{1,0:T(8,128)(2,1)} %he_hbm.1, bf16[768,768]{1,0:T(8,128)(2,1)} %ho_hbm.1, bf16[768,768]{1,0:T(8,128)(2,1)} %de_hbm.1, ...), custom_call_target="tpu_custom_call" | custom-call | tf_op jit(solution)/shard_map/pallas_call | solution.py:282
  96.1 1.6 %copy.11 = bf16[2,8,24,256]{3,2,1,0:T(8,128)(2,1)} copy(bf16[2,8,24,256]{3,2,1,0:T(8,128)(2,1)} %bitcast.6) | data formatting | bytes 393216
  97.7 1.6 %copy.12 = bf16[2,8,24,256]{3,2,1,0:T(8,128)(2,1)} copy(bf16[2,8,24,256]{3,2,1,0:T(8,128)(2,1)} %bitcast.5) | data formatting | bytes 393216

commit v2 on v1

v2 whole, which is shorter than its diff:
```python
import jax
import jax.numpy as jnp
from jax import lax
from jax.experimental import pallas as pl
from jax.experimental.pallas import tpu as pltpu
from jax.sharding import PartitionSpec as P

NY = 1536
KZ = 4096
XMODES = 5120
KX = 8
HALF = NY // 2
NX = 4
NZ = 16
NQ = 16
NJ = NZ // NQ
NG = 8
NB = 24
NL = 128
NC = 2
OWN = NQ * NB
NR = NJ * NC
MESH = pl.DeviceIdType.MESH
f32, bf16 = jnp.float32, jnp.bfloat16


def kernel(
    v_hbm, kx_ref, kz_ref, he_hbm, ho_hbm, de_hbm, do_hbm,
    outu_ref, outd_ref,
    v_scr, rx, tx, rxo, he, ho, de, do, hes, hos, e1, e2, e3, e4,
    loc_sem, w_sem, entered, zs, zr, xs, xr, bs, br, es1, er1, es2, er2, es3, er3, es4, er4,
):
    wall = lax.axis_index("wall")
    span = lax.axis_index("span")
    x, z = wall // NZ, wall % NZ
    yy, zh, core = span // 4, (span // 2) % 2, span % 2
    yc = yy * 2 + core
    half = z // NQ

    def at_z(p):
        return (x * NZ + p, span)

    def at_x(d):
        return (((x + d) % NX) * NZ + z, span)

    def at_yc(d):
        t = (yc + d) % 8
        return (wall, ((t // 2) * 2 + zh) * 2 + t % 2)

    across = (x * NZ + (NZ - 1 - z), (yy * 2 + (1 - zh)) * 2 + core)

    vcopies = [
        pltpu.make_async_copy(v_hbm.at[:, :, pl.ds(h * NL, NL)], v_scr.at[:, h], loc_sem.at[h]) for h in range(NC)
    ]
    m = x // 2
    plane0 = NZ * NB * x + OWN * half
    i0 = (1 - m) * plane0 + m * (NY - OWN - plane0)
    i0 = pl.multiple_of(i0, OWN)
    wcopies = [
        pltpu.make_async_copy(he_hbm, he, w_sem.at[0]),
        pltpu.make_async_copy(ho_hbm, ho, w_sem.at[1]),
        pltpu.make_async_copy(de_hbm.at[pl.ds(i0, OWN), :], de, w_sem.at[2]),
        pltpu.make_async_copy(do_hbm.at[pl.ds(i0, OWN), :], do, w_sem.at[3]),
    ]

    barrier = pltpu.get_barrier_semaphore()

    def greet(dev):
        pl.semaphore_signal(barrier, inc=1, device_id=dev, device_id_type=MESH)

    def greet_up(p, carry):
        greet(at_z(p))
        return carry

    lax.fori_loop(z + 1, NZ, greet_up, 0)

    @pl.when(zh == 0)
    def _():
        greet(across)

    for d in range(1, NX):
        greet(at_x(d))
    for d in range(1, 8):
        greet(at_yc(d))
    for c in vcopies + wcopies:
        c.start()

    for c in vcopies:
        c.wait()
    part = jnp.zeros((8, NL), f32)
    for c in range(NZ):
        for h in range(NC):
            w = v_scr[c, h].astype(f32)
            w = w * w
            part = part + (w[0:8] + w[8:16] + w[16:24])
    e1[yc] = jnp.sum(part, axis=0, keepdims=True)

    pl.semaphore_wait(barrier, z + zh + (NX - 1) + 7)

    def zcopy(r, p):
        j, h = r // NC, r % NC
        return pltpu.make_async_remote_copy(
            src_ref=v_scr.at[NJ * (p % NQ) + j, h], dst_ref=rx.at[r, x * NZ + z],
            send_sem=zs.at[r, p], recv_sem=zr.at[r, z],
            device_id=at_z(p), device_id_type=MESH,
        )

    def zwait(r, q):
        pltpu.make_async_remote_copy(
            src_ref=v_scr.at[0, 0], dst_ref=rx.at[r, x * NZ + q],
            send_sem=zs.at[r, q], recv_sem=zr.at[r, q],
            device_id=across, device_id_type=MESH,
        ).wait_recv()

    def tell(i, carry):
        pl.semaphore_signal(entered.at[z], inc=1, device_id=at_z(z - 1 - i), device_id_type=MESH)
        return carry

    lax.fori_loop(0, z, tell, 0)

    @pl.when(zh == 1)
    def _():
        pl.semaphore_signal(entered.at[NZ], inc=1, device_id=across, device_id_type=MESH)

    for r in range(NR):
        lax.fori_loop(0, z, lambda p, c, r=r: (zcopy(r, p).start(), c)[1], 0)

    def ecopy(buf, slot, ss, rs, dev):
        return pltpu.make_async_remote_copy(
            src_ref=buf.at[slot], dst_ref=buf.at[slot], send_sem=ss, recv_sem=rs,
            device_id=dev, device_id_type=MESH,
        )

    for d in range(1, 8):
        ecopy(e1, yc, es1.at[d], er1.at[yc], at_yc(d)).start()

    for d in range(1, 8):
        ecopy(e1, (yc + d) % 8, es1.at[d], er1.at[(yc + d) % 8], across).wait_recv()
    e2[x] = jnp.sum(e1[...], axis=0)
    for d in range(1, NX):
        ecopy(e2, x, es2.at[d], er2.at[x], at_x(d)).start()
    for d in range(1, NX):
        ecopy(e2, (x + d) % NX, es2.at[d], er2.at[(x + d) % NX], across).wait_recv()
    e3[zh] = jnp.sum(e2[...], axis=0)

    @pl.when(zh == 1)
    def _():
        ecopy(e3, zh, es3.at[0], er3.at[zh], across).start()

    def send_up(p, carry):
        pl.semaphore_wait(entered.at[p], 1)
        for r in range(NR // 2):
            zcopy(r, p).start()
        return carry

    lax.fori_loop(z + 1, NZ, send_up, 0)
    for r in range(NR // 2, NR):
        lax.fori_loop(0, NZ - 1 - z, lambda i, c, r=r: (zcopy(r, NZ - 1 - i).start(), c)[1], 0)
    for r in range(NR):
        pltpu.make_async_copy(v_scr.at[NJ * (z % NQ) + r // NC, r % NC], rx.at[r, x * NZ + z], zr.at[r, z]).start()

    @pl.when(zh == 0)
    def _():
        pl.semaphore_wait(entered.at[NZ], 1)
        ecopy(e3, zh, es3.at[0], er3.at[zh], across).start()

    rows = lax.broadcasted_iota(jnp.int32, (256, 256), 0)
    cols = lax.broadcasted_iota(jnp.int32, (256, 256), 1)
    flip256 = jnp.where(rows + cols == 255, 1.0, 0.0).astype(bf16)
    rows = lax.broadcasted_iota(jnp.int32, (OWN, OWN), 0)
    cols = lax.broadcasted_iota(jnp.int32, (OWN, OWN), 1)
    flip_own = jnp.where(rows + cols == OWN - 1, 1.0, 0.0).astype(bf16)
    mirrored = x >= 2
    sign = jnp.where(mirrored, -1.0, 1.0).astype(f32)

    def group(g):
        return ((z // NG + g) % 2) * NG

    def xcopy(r, g, d):
        blocks = pl.ds(x * NZ + group(g), NG)
        return pltpu.make_async_remote_copy(
            src_ref=rx.at[r, blocks], dst_ref=rx.at[r, blocks],
            send_sem=xs.at[r, g, d], recv_sem=xr.at[r, g, d],
            device_id=at_x(d), device_id_type=MESH,
        )

    def xwait(r, g, d):
        blocks = pl.ds(((x + NX - d) % NX) * NZ + group(g), NG)
        pltpu.make_async_remote_copy(
            src_ref=rx.at[r, blocks], dst_ref=rx.at[r, blocks],
            send_sem=xs.at[r, g, d], recv_sem=xr.at[r, g, d],
            device_id=at_x(d), device_id_type=MESH,
        ).wait_recv()

    def bcopy(r, d):
        p = (z + d) % NQ
        return pltpu.make_async_remote_copy(
            src_ref=tx.at[r, p], dst_ref=rxo.at[r, z % NQ],
            send_sem=bs.at[r, d], recv_sem=br.at[r, z % NQ],
            device_id=at_z(half * NQ + p), device_id_type=MESH,
        )

    def compute(r):
        lo = rx[r, 0:32].astype(f32).reshape(HALF, NL)
        hi = rx[r, 32:64].astype(f32).reshape(HALF, NL).astype(bf16)
        fl = jnp.concatenate(
            [jnp.dot(flip256, hi[HALF - 256 * (b + 1):HALF - 256 * b], preferred_element_type=f32) for b in range(3)],
            axis=0,
        )
        even = ((lo + fl) * 0.5).astype(bf16)
        odd = ((lo - fl) * 0.5).astype(bf16)
        heven = jnp.dot(he[...], even, preferred_element_type=f32).astype(bf16)
        hodd = jnp.dot(ho[...], odd, preferred_element_type=f32).astype(bf16)
        hes[...] = heven
        hos[...] = hodd
        dodd = jnp.dot(de[...], heven, preferred_element_type=f32)
        deven = jnp.dot(do[...], hodd, preferred_element_type=f32)
        he32 = hes[pl.ds(i0, OWN), :].astype(f32)
        ho32 = hos[pl.ds(i0, OWN), :].astype(f32)

        def place(t, lines):
            back = jnp.dot(flip_own, lines, preferred_element_type=f32)
            res = jnp.where(mirrored, back, lines.astype(f32))
            tx[r, :, t] = res.reshape(NQ, NB, NL).astype(bf16)

        place(0, (he32 + sign * ho32).astype(bf16))
        place(1, (deven + sign * dodd).astype(bf16))

    for r in range(NR):
        for g in range(2):
            lax.fori_loop(0, NG, lambda q, c, g=g: (zwait(r, group(g) + q), c)[1], 0)
            for d in range(1, NX):
                xcopy(r, g, d).start()
        if r == 0:
            for c in wcopies:
                c.wait()
            ecopy(e3, 1 - zh, es3.at[0], er3.at[1 - zh], across).wait_recv()
            e4[z] = jnp.sum(e3[...], axis=0)

            def send_e4(d, carry):
                ecopy(e4, z, es4.at[d], er4.at[z], at_z((z + d) % NZ)).start()
                return carry

            lax.fori_loop(1, NZ, send_e4, 0)
        for g in range(2):
            for d in range(1, NX):
                xwait(r, g, d)
        compute(r)

        def send_back(i, carry):
            bcopy(r, NQ // 2 - i).start()

            @pl.when(i > 0)
            def _():
                bcopy(r, NQ // 2 + i).start()
            return carry

        lax.fori_loop(0, NQ // 2, send_back, 0)
        pltpu.make_async_copy(tx.at[r, z % NQ], rxo.at[r, z % NQ], br.at[r, z % NQ]).start()

    kz = kz_ref[...].astype(f32) / KZ
    kz_sq = kz * kz

    def wait_e4(d, carry):
        p = (z + d) % NZ
        ecopy(e4, p, es4.at[d], er4.at[p], across).wait_recv()
        return carry

    lax.fori_loop(1, NZ, wait_e4, 0)
    energy = jnp.sum(jnp.sum(e4[...], axis=0), axis=1, keepdims=True)
    scale = jnp.float32(2.0 * KX * NY * KZ) / energy
    factors = []
    for k in range(KX):
        kx = kx_ref[k].astype(f32) / XMODES
        factors.append(scale * (1.0 / (1.0 + 2.0 * (kx * kx + kz_sq))))

    def bwait(r, q):
        pltpu.make_async_remote_copy(
            src_ref=tx.at[r, q], dst_ref=rxo.at[r, q],
            send_sem=bs.at[r, 0], recv_sem=br.at[r, q],
            device_id=across, device_id_type=MESH,
        ).wait_recv()

    for r in range(NR):
        j, h = r // NC, r % NC
        lax.fori_loop(0, NQ, lambda q, carry: (bwait(r, q), carry)[1], 0)
        for q in range(NQ):
            c = NJ * q + j
            f = factors[c % KX][:, h * NL:(h + 1) * NL]
            for t, out in enumerate((outu_ref, outd_ref)):
                out[c, :, h * NL:(h + 1) * NL] = (f * rxo[r, q, t].astype(f32)).astype(bf16)

    def drain_z(d, carry):
        for r in range(NR):
            zcopy(r, (z + d) % NZ).wait_send()
        return carry

    lax.fori_loop(1, NZ, drain_z, 0)

    def drain_b(d, carry):
        for r in range(NR):
            bcopy(r, d).wait_send()
        return carry

    lax.fori_loop(1, NQ, drain_b, 0)
    for d in range(1, NX):
        for r in range(NR):
            for g in range(2):
                xcopy(r, g, d).wait_send()
        ecopy(e2, x, es2.at[d], er2.at[x], at_x(d)).wait_send()
    for d in range(1, 8):
        ecopy(e1, yc, es1.at[d], er1.at[yc], at_yc(d)).wait_send()

    ecopy(e3, zh, es3.at[0], er3.at[zh], across).wait_send()

    def drain_e4(d, carry):
        ecopy(e4, z, es4.at[d], er4.at[z], at_z((z + d) % NZ)).wait_send()
        return carry

    lax.fori_loop(1, NZ, drain_e4, 0)


def local(velocity, kx_index, kz_index, helm_even, helm_odd, deriv_even, deriv_odd):
    v = velocity.reshape(NZ, NB, NC * NL)
    vm = pl.BlockSpec(memory_space=pltpu.VMEM)
    hbm = pl.BlockSpec(memory_space=pl.ANY)
    shape = jax.ShapeDtypeStruct((NZ, NB, NC * NL), bf16)
    dma = pltpu.SemaphoreType.DMA
    outu, outd = pl.pallas_call(
        kernel,
        out_shape=(shape, shape),
        in_specs=[hbm, pl.BlockSpec(memory_space=pltpu.SMEM), vm, hbm, hbm, hbm, hbm],
        out_specs=(vm, vm),
        scratch_shapes=[
            pltpu.VMEM((NZ, NC, NB, NL), bf16),
            pltpu.VMEM((NR, NX * NZ, NB, NL), bf16),
            pltpu.VMEM((NR, NQ, 2, NB, NL), bf16),
            pltpu.VMEM((NR, NQ, 2, NB, NL), bf16),
            pltpu.VMEM((HALF, HALF), bf16),
            pltpu.VMEM((HALF, HALF), bf16),
            pltpu.VMEM((OWN, HALF), bf16),
            pltpu.VMEM((OWN, HALF), bf16),
            pltpu.VMEM((HALF, NL), bf16),
            pltpu.VMEM((HALF, NL), bf16),
            pltpu.VMEM((8, 1, NL), f32),
            pltpu.VMEM((NX, 1, NL), f32),
            pltpu.VMEM((2, 1, NL), f32),
            pltpu.VMEM((NZ, 1, NL), f32),
            dma((NC,)), dma((4,)), pltpu.SemaphoreType.REGULAR((NZ + 1,)),
            dma((NR, NZ)), dma((NR, NZ)),
            dma((NR, 2, NX)), dma((NR, 2, NX)),
            dma((NR, NQ)), dma((NR, NQ)),
            dma((8,)), dma((8,)), dma((NX,)), dma((NX,)),
            dma((1,)), dma((2,)), dma((NZ,)), dma((NZ,)),
        ],
        compiler_params=pltpu.CompilerParams(collective_id=0, has_side_effects=True),
    )(v, kx_index, kz_index.reshape(1, NC * NL), helm_even, helm_odd, deriv_even, deriv_odd)
    full = (2, KX, NB, NC * NL)
    return outu.reshape(full), outd.reshape(full)


def solution(mesh):
    in_specs = (P(None, None, "wall", "span"), P(), P("span"), P(), P(), P(), P())
    out_specs = (P(None, None, "wall", "span"), P(None, None, "wall", "span"))
    return jax.shard_map(local, mesh=mesh, in_specs=in_specs, out_specs=out_specs, check_vma=False)
```

time: 99.5 us -> 87.9 us (0.88)
  the two profiles are of different devices: /device:TPU:16 before, /device:TPU:1 now
where the time goes in v2:
time: 87.9 us; the launch traced here: 86.2 us
  Pallas kernels  82.3 us (94%)
  local copies, waits for them, and re-layouts  3.23 us (4%)
    pallas_call x1, Pallas kernels, local(): pl.pallas_call(kernel, out_shape=(shape, shape), in_specs=[hbm, pl.BlockS...  82.3 us
    unnamed x2, local copies, waits for them, and re-layouts  3.23 us

profile of v2, /device:TPU:1, one launch (start us, length us, event | category | flops | bytes accessed | tf_op | source)
XLA Modules:
  0.0 86.2 jit_solution(13892155073533365421)
XLA Ops:
  0.6 82.3 %shard_map.86 = (bf16[16,24,256]{2,1,0:T(8,128)(2,1)}, bf16[16,24,256]{2,1,0:T(8,128)(2,1)}) custom-call(bf16[16,24,256]{2,1,0:T(8,128)(2,1)} %bitcast.4, s32[8]{0:T(128)} %kx_ref.1, s32[1,256]{1,0:T(1,128)} %bitcast.7, bf16[768,768]{1,0:T(8,128)(2,1)} %he_hbm.1, bf16[768,768]{1,0:T(8,128)(2,1)} %ho_hbm.1, bf16[768,768]{1,0:T(8,128)(2,1)} %de_hbm.1, ...), custom_call_target="tpu_custom_call" | custom-call | tf_op jit(solution)/shard_map/pallas_call | solution.py:329
  83.0 1.6 %copy.11 = bf16[2,8,24,256]{3,2,1,0:T(8,128)(2,1)} copy(bf16[2,8,24,256]{3,2,1,0:T(8,128)(2,1)} %bitcast.6) | data formatting | bytes 393216
  84.6 1.6 %copy.12 = bf16[2,8,24,256]{3,2,1,0:T(8,128)(2,1)} copy(bf16[2,8,24,256]{3,2,1,0:T(8,128)(2,1)} %bitcast.5) | data formatting | bytes 393216

commit v3 on v2

--- a/solution.py
+++ b/solution.py
@@ -12,14 +12,15 @@
 HALF = NY // 2
 NX = 4
 NZ = 16
-NQ = 16
-NJ = NZ // NQ
-NG = 8
+NG = 4
+NLATE = 2
+E0 = 4
 NB = 24
 NL = 128
 NC = 2
-OWN = NQ * NB
-NR = NJ * NC
+OWN = NZ * NB
+NR = NC
+NE = NLATE * NC
 MESH = pl.DeviceIdType.MESH
 f32, bf16 = jnp.float32, jnp.bfloat16
 
@@ -35,7 +36,9 @@
     x, z = wall // NZ, wall % NZ
     yy, zh, core = span // 4, (span // 2) % 2, span % 2
     yc = yy * 2 + core
-    half = z // NQ
+    n_own = NZ - NLATE * (1 - zh)
+    owner = z < n_own
+    extra = (zh == 0) & (z >= E0) & (z < E0 + NE)
 
     def at_z(p):
         return (x * NZ + p, span)
@@ -53,7 +56,7 @@
         pltpu.make_async_copy(v_hbm.at[:, :, pl.ds(h * NL, NL)], v_scr.at[:, h], loc_sem.at[h]) for h in range(NC)
     ]
     m = x // 2
-    plane0 = NZ * NB * x + OWN * half
+    plane0 = OWN * x
     i0 = (1 - m) * plane0 + m * (NY - OWN - plane0)
     i0 = pl.multiple_of(i0, OWN)
     wcopies = [
@@ -97,10 +100,16 @@
 
     pl.semaphore_wait(barrier, z + zh + (NX - 1) + 7)
 
+    def block(r, p):
+        if r < NR:
+            return p, r
+        t = p - E0
+        return NZ - NLATE + t // NC, t % NC
+
     def zcopy(r, p):
-        j, h = r // NC, r % NC
+        c, h = block(r, p)
         return pltpu.make_async_remote_copy(
-            src_ref=v_scr.at[NJ * (p % NQ) + j, h], dst_ref=rx.at[r, x * NZ + z],
+            src_ref=v_scr.at[c, h], dst_ref=rx.at[r, x * NZ + z],
             send_sem=zs.at[r, p], recv_sem=zr.at[r, z],
             device_id=at_z(p), device_id_type=MESH,
         )
@@ -122,8 +131,21 @@
     def _():
         pl.semaphore_signal(entered.at[NZ], inc=1, device_id=across, device_id_type=MESH)
 
-    for r in range(NR):
-        lax.fori_loop(0, z, lambda p, c, r=r: (zcopy(r, p).start(), c)[1], 0)
+    def for_owners(r, do, below, far=False):
+        if r < NR:
+            first, end = (0, jnp.minimum(z, n_own)) if below else (z + 1, n_own)
+        else:
+            first, end = (E0, jnp.minimum(z, E0 + NE)) if below else (jnp.maximum(z + 1, E0), E0 + NE)
+            end = jnp.where(zh == 0, end, first)
+
+        def body(p, carry):
+            do(end - 1 + first - p if far else p)
+            return carry
+
+        lax.fori_loop(first, end, body, 0)
+
+    for r in range(NR + 1):
+        for_owners(r, lambda p: zcopy(r, p).start(), True)
 
     def ecopy(buf, slot, ss, rs, dev):
         return pltpu.make_async_remote_copy(
@@ -149,20 +171,15 @@
 
     def send_up(p, carry):
         pl.semaphore_wait(entered.at[p], 1)
-        for r in range(NR // 2):
-            zcopy(r, p).start()
+
+        @pl.when(p < n_own)
+        def _():
+            zcopy(0, p).start()
         return carry
 
     lax.fori_loop(z + 1, NZ, send_up, 0)
-    for r in range(NR // 2, NR):
-        lax.fori_loop(0, NZ - 1 - z, lambda i, c, r=r: (zcopy(r, NZ - 1 - i).start(), c)[1], 0)
-    for r in range(NR):
-        pltpu.make_async_copy(v_scr.at[NJ * (z % NQ) + r // NC, r % NC], rx.at[r, x * NZ + z], zr.at[r, z]).start()
-
-    @pl.when(zh == 0)
-    def _():
-        pl.semaphore_wait(entered.at[NZ], 1)
-        ecopy(e3, zh, es3.at[0], er3.at[zh], across).start()
+    for r in range(1, NR + 1):
+        for_owners(r, lambda p: zcopy(r, p).start(), False, True)
 
     rows = lax.broadcasted_iota(jnp.int32, (256, 256), 0)
     cols = lax.broadcasted_iota(jnp.int32, (256, 256), 1)
@@ -174,7 +191,8 @@
     sign = jnp.where(mirrored, -1.0, 1.0).astype(f32)
 
     def group(g):
-        return ((z // NG + g) % 2) * NG
+        own, up = z // NG, z // NG // 2
+        return (own, 1 - own + 4 * up, 2 - up, 3 - 3 * up)[g] * NG
 
     def xcopy(r, g, d):
         blocks = pl.ds(x * NZ + group(g), NG)
@@ -192,12 +210,12 @@
             device_id=at_x(d), device_id_type=MESH,
         ).wait_recv()
 
-    def bcopy(r, d):
-        p = (z + d) % NQ
+    def bcopy(r, p):
+        c, h = block(r, z)
         return pltpu.make_async_remote_copy(
-            src_ref=tx.at[r, p], dst_ref=rxo.at[r, z % NQ],
-            send_sem=bs.at[r, d], recv_sem=br.at[r, z % NQ],
-            device_id=at_z(half * NQ + p), device_id_type=MESH,
+            src_ref=tx.at[r, p], dst_ref=rxo.at[h, c],
+            send_sem=bs.at[r, p], recv_sem=br.at[h, c],
+            device_id=at_z(p), device_id_type=MESH,
         )
 
     def compute(r):
@@ -221,42 +239,71 @@
         def place(t, lines):
             back = jnp.dot(flip_own, lines, preferred_element_type=f32)
             res = jnp.where(mirrored, back, lines.astype(f32))
-            tx[r, :, t] = res.reshape(NQ, NB, NL).astype(bf16)
+            tx[r, :, t] = res.reshape(NZ, NB, NL).astype(bf16)
 
         place(0, (he32 + sign * ho32).astype(bf16))
         place(1, (deven + sign * dodd).astype(bf16))
 
-    for r in range(NR):
-        for g in range(2):
-            lax.fori_loop(0, NG, lambda q, c, g=g: (zwait(r, group(g) + q), c)[1], 0)
+    def energy_on():
+        @pl.when(zh == 0)
+        def _():
+            pl.semaphore_wait(entered.at[NZ], 1)
+            ecopy(e3, zh, es3.at[0], er3.at[zh], across).start()
+
+        ecopy(e3, 1 - zh, es3.at[0], er3.at[1 - zh], across).wait_recv()
+        e4[z] = jnp.sum(e3[...], axis=0)
+
+        def send_e4(d, carry):
+            ecopy(e4, z, es4.at[d], er4.at[z], at_z((z + d) % NZ)).start()
+            return carry
+
+        lax.fori_loop(1, NZ, send_e4, 0)
+
+    def round_of(r):
+        c, h = block(r, z)
+        pltpu.make_async_copy(v_scr.at[c, h], rx.at[r, x * NZ + z], zr.at[r, z]).start()
+        for g in range(NZ // NG):
+            lax.fori_loop(0, NG, lambda q, cc, g=g: (zwait(r, group(g) + q), cc)[1], 0)
             for d in range(1, NX):
                 xcopy(r, g, d).start()
         if r == 0:
-            for c in wcopies:
-                c.wait()
-            ecopy(e3, 1 - zh, es3.at[0], er3.at[1 - zh], across).wait_recv()
-            e4[z] = jnp.sum(e3[...], axis=0)
-
-            def send_e4(d, carry):
-                ecopy(e4, z, es4.at[d], er4.at[z], at_z((z + d) % NZ)).start()
-                return carry
-
-            lax.fori_loop(1, NZ, send_e4, 0)
-        for g in range(2):
+            for w in wcopies:
+                w.wait()
+        for g in range(NZ // NG):
             for d in range(1, NX):
                 xwait(r, g, d)
         compute(r)
 
         def send_back(i, carry):
-            bcopy(r, NQ // 2 - i).start()
-
-            @pl.when(i > 0)
+            k = NZ - 1 - i
+
+            @pl.when(z >= k)
             def _():
-                bcopy(r, NQ // 2 + i).start()
+                bcopy(r, z - k).start()
+
+            @pl.when(z + k < NZ)
+            def _():
+                bcopy(r, z + k).start()
             return carry
 
-        lax.fori_loop(0, NQ // 2, send_back, 0)
-        pltpu.make_async_copy(tx.at[r, z % NQ], rxo.at[r, z % NQ], br.at[r, z % NQ]).start()
+        lax.fori_loop(0, NZ - 1, send_back, 0)
+        pltpu.make_async_copy(tx.at[r, z], rxo.at[h, c], br.at[h, c]).start()
+
+    @pl.when(owner)
+    def _():
+        round_of(0)
+        energy_on()
+        round_of(1)
+
+    @pl.when(extra)
+    def _():
+        round_of(NR)
+
+    @pl.when(jnp.logical_not(owner))
+    def _():
+        for w in wcopies:
+            w.wait()
+        energy_on()
 
     kz = kz_ref[...].astype(f32) / KZ
     kz_sq = kz * kz
@@ -282,31 +329,34 @@
         ).wait_recv()
 
     for r in range(NR):
-        j, h = r // NC, r % NC
-        lax.fori_loop(0, NQ, lambda q, carry: (bwait(r, q), carry)[1], 0)
-        for q in range(NQ):
-            c = NJ * q + j
+        h = r
+        lax.fori_loop(0, NZ, lambda q, carry: (bwait(r, q), carry)[1], 0)
+        for q in range(NZ):
+            c = q
             f = factors[c % KX][:, h * NL:(h + 1) * NL]
             for t, out in enumerate((outu_ref, outd_ref)):
                 out[c, :, h * NL:(h + 1) * NL] = (f * rxo[r, q, t].astype(f32)).astype(bf16)
 
-    def drain_z(d, carry):
+    for r in range(NR + 1):
+        for_owners(r, lambda p: zcopy(r, p).wait_send(), True)
+        for_owners(r, lambda p: zcopy(r, p).wait_send(), False)
+
+    def drain_round(r):
+        lax.fori_loop(1, NZ, lambda d, cc: (bcopy(r, (z + d) % NZ).wait_send(), cc)[1], 0)
+        for d in range(1, NX):
+            for g in range(NZ // NG):
+                xcopy(r, g, d).wait_send()
+
+    @pl.when(owner)
+    def _():
         for r in range(NR):
-            zcopy(r, (z + d) % NZ).wait_send()
-        return carry
-
-    lax.fori_loop(1, NZ, drain_z, 0)
-
-    def drain_b(d, carry):
-        for r in range(NR):
-            bcopy(r, d).wait_send()
-        return carry
-
-    lax.fori_loop(1, NQ, drain_b, 0)
+            drain_round(r)
+
+    @pl.when(extra)
+    def _():
+        drain_round(NR)
+
     for d in range(1, NX):
-        for r in range(NR):
-            for g in range(2):
-                xcopy(r, g, d).wait_send()
         ecopy(e2, x, es2.at[d], er2.at[x], at_x(d)).wait_send()
     for d in range(1, 8):
         ecopy(e1, yc, es1.at[d], er1.at[yc], at_yc(d)).wait_send()
@@ -318,6 +368,17 @@
         return carry
 
     lax.fori_loop(1, NZ, drain_e4, 0)
+
+
+def settle(u_ref, d_ref, outu_ref, outd_ref, sem):
+    copies = [
+        pltpu.make_async_copy(u_ref, outu_ref, sem.at[0]),
+        pltpu.make_async_copy(d_ref, outd_ref, sem.at[1]),
+    ]
+    for c in copies:
+        c.start()
+    for c in copies:
+        c.wait()
 
 
 def local(velocity, kx_index, kz_index, helm_even, helm_odd, deriv_even, deriv_odd):
@@ -328,14 +389,14 @@
     dma = pltpu.SemaphoreType.DMA
     outu, outd = pl.pallas_call(
         kernel,
-        out_shape=(shape, shape),
+        out_shape=(pltpu.VMEM((NZ, NB, NC * NL), bf16),) * 2,
         in_specs=[hbm, pl.BlockSpec(memory_space=pltpu.SMEM), vm, hbm, hbm, hbm, hbm],
         out_specs=(vm, vm),
         scratch_shapes=[
             pltpu.VMEM((NZ, NC, NB, NL), bf16),
-            pltpu.VMEM((NR, NX * NZ, NB, NL), bf16),
-            pltpu.VMEM((NR, NQ, 2, NB, NL), bf16),
-            pltpu.VMEM((NR, NQ, 2, NB, NL), bf16),
+            pltpu.VMEM((NR + 1, NX * NZ, NB, NL), bf16),
+            pltpu.VMEM((NR + 1, NZ, 2, NB, NL), bf16),
+            pltpu.VMEM((NR, NZ, 2, NB, NL), bf16),
             pltpu.VMEM((HALF, HALF), bf16),
             pltpu.VMEM((HALF, HALF), bf16),
             pltpu.VMEM((OWN, HALF), bf16),
@@ -347,14 +408,18 @@
             pltpu.VMEM((2, 1, NL), f32),
             pltpu.VMEM((NZ, 1, NL), f32),
             dma((NC,)), dma((4,)), pltpu.SemaphoreType.REGULAR((NZ + 1,)),
-            dma((NR, NZ)), dma((NR, NZ)),
-            dma((NR, 2, NX)), dma((NR, 2, NX)),
-            dma((NR, NQ)), dma((NR, NQ)),
+            dma((NR + 1, NZ)), dma((NR + 1, NZ)),
+            dma((NR + 1, NZ // NG, NX)), dma((NR + 1, NZ // NG, NX)),
+            dma((NR + 1, NZ)), dma((NR, NZ)),
             dma((8,)), dma((8,)), dma((NX,)), dma((NX,)),
             dma((1,)), dma((2,)), dma((NZ,)), dma((NZ,)),
         ],
         compiler_params=pltpu.CompilerParams(collective_id=0, has_side_effects=True),
     )(v, kx_index, kz_index.reshape(1, NC * NL), helm_even, helm_odd, deriv_even, deriv_odd)
+    outu, outd = pl.pallas_call(
+        settle, out_shape=(shape, shape), in_specs=[hbm, hbm], out_specs=(hbm, hbm),
+        scratch_shapes=[dma((2,))], compiler_params=pltpu.CompilerParams(vmem_limit_bytes=2 ** 20),
+    )(outu, outd)
     full = (2, KX, NB, NC * NL)
     return outu.reshape(full), outd.reshape(full)
 

time: 87.9 us -> 78.7 us (0.90)
  the two profiles are of different devices: /device:TPU:1 before, /device:TPU:256 now
where the time goes in v3:
time: 78.7 us; the launch traced here: 78.5 us
  Pallas kernels  77.9 us (99%)
    pallas_call x1, Pallas kernels, local(): pl.pallas_call(kernel, out_shape=(pltpu.VMEM((NZ, NB, NC * NL), bf16),) *...  77.1 us

profile of v3, /device:TPU:256, one launch (start us, length us, event | category | flops | bytes accessed | tf_op | source)
XLA Modules:
  0.0 78.5 jit_solution(12382014152524387291)
XLA Ops:
  0.6 77.1 %shard_map.86 = (bf16[16,24,256]{2,1,0:T(8,128)(2,1)S(1)}, bf16[16,24,256]{2,1,0:T(8,128)(2,1)S(1)}) custom-call(bf16[16,24,256]{2,1,0:T(8,128)(2,1)} %bitcast.4, s32[8]{0:T(128)} %kx_ref.1, s32[1,256]{1,0:T(1,128)} %bitcast.5, bf16[768,768]{1,0:T(8,128)(2,1)} %he_hbm.1, bf16[768,768]{1,0:T(8,128)(2,1)} %ho_hbm.1, bf16[768,768]{1,0:T(8,128)(2,1)} %de_hbm.1, ...), custom_call_target="tpu_custom_call" | custom-call | tf_op jit(solution)/shard_map/pallas_call | solution.py:390
  77.7 0.8 shard_map.87

commit v4 on v3

--- a/solution.py
+++ b/solution.py
@@ -14,7 +14,7 @@
 NZ = 16
 NG = 4
 NLATE = 2
-E0 = 4
+E0 = 5
 NB = 24
 NL = 128
 NC = 2

time: 78.7 us -> 77.5 us (0.985)
  the two profiles are of different devices: /device:TPU:256 before, /device:TPU:928 now
where the time goes in v4:
time: 77.5 us; the launch traced here: 77.3 us
  Pallas kernels  76.7 us (99%)
    pallas_call x1, Pallas kernels, local(): pl.pallas_call(kernel, out_shape=(pltpu.VMEM((NZ, NB, NC * NL), bf16),) *...  75.9 us

profile of v4, /device:TPU:928, one launch (start us, length us, event | category | flops | bytes accessed | tf_op | source)
XLA Modules:
  0.0 77.3 jit_solution(16151672882412617116)
XLA Ops:
  0.6 75.9 %shard_map.86 = (bf16[16,24,256]{2,1,0:T(8,128)(2,1)S(1)}, bf16[16,24,256]{2,1,0:T(8,128)(2,1)S(1)}) custom-call(bf16[16,24,256]{2,1,0:T(8,128)(2,1)} %bitcast.4, s32[8]{0:T(128)} %kx_ref.1, s32[1,256]{1,0:T(1,128)} %bitcast.5, bf16[768,768]{1,0:T(8,128)(2,1)} %he_hbm.1, bf16[768,768]{1,0:T(8,128)(2,1)} %ho_hbm.1, bf16[768,768]{1,0:T(8,128)(2,1)} %de_hbm.1, ...), custom_call_target="tpu_custom_call" | custom-call | tf_op jit(solution)/shard_map/pallas_call | solution.py:390
  76.5 0.8 shard_map.87
